TPU v7x, 256 devices: a whole 4x4x8 slice. The times are simulated.
256 devices in a mesh: row: 8 (over y, core), col: 32 (over z, x).
Axes of the slice: x: 4, y: 4, z: 8, core: 2. Of those that a mesh axis runs over, the one named last changes fastest.
Arguments:
- amps: bfloat16 [1024, 256, 256], P('row', 'col'), may hold values from -6 to 6
- ints: bfloat16 [16384, 256, 256], P(('row', 'col')), may hold values from -0.0234375 to 0.0234375
- task_cd: int32 [16384], P(('row', 'col')), may hold values from 0 to 7, as said below
- task_ab: int32 [16384], P(('row', 'col')), may hold values from 0 to 7
- task_count: int32 [256], P(('row', 'col')), may hold values from 8 to 64, as said below
Outputs:
- residual: bfloat16 [1024, 64, 256], P('col', 'row')
Inputs may be any that keep to these rules, and one draw needn't show every extreme that they name: On each device the slots name distinct (task_cd, task_ab) pairs. The live slots of a device are its first task_count ones; some device has all 64 slots live in every draw.
All inputs are finite; a program needn't handle non-finite values.
Results may differ from a plain program's by a relative error of at most 0.001.
Values may be sent and summed in bfloat16 or wider, within the bound.
A program may use at most 128 MiB of HBM per device.

v0:
```python
import jax
import jax.numpy as jnp
from jax import lax
from jax.sharding import Mesh
from jax.sharding import PartitionSpec as P

CD_COL = 8
PAIR_TILES_ROW = 8
COL = ("col_0", "col_1")
ROW_COL = ("row", "col_0", "col_1")


def sum_by_axis(value, axes, dim):
    for axis in axes:
        value = lax.psum_scatter(value, axis, scatter_dimension=dim, tiled=True)
    return value


def dense_tiles(ints, task_cd, task_ab, count):
    slots = ints.shape[0]
    order = jnp.arange(slots, dtype=jnp.int32)
    live = order < count
    wanted = jnp.arange(PAIR_TILES_ROW * CD_COL, dtype=jnp.int32)[:, None]
    slot_key = task_ab * CD_COL + task_cd
    match = (slot_key[None, :] == wanted) & live[None, :]
    found = jnp.sum(jnp.where(match, order[None, :], 0), axis=1)
    present_mask = jnp.any(match, axis=1)
    table = jnp.take(ints, found, axis=0) * present_mask.astype(ints.dtype)[:, None, None]
    return table.reshape(PAIR_TILES_ROW, CD_COL, ints.shape[1], ints.shape[2])


def ladder_term(rows_amps, table):
    return jnp.einsum("nkt,aktu->nau", rows_amps, table, preferred_element_type=jnp.float32)


def shards(amps, ints, task_cd, task_ab, task_count):
    whole = lax.all_gather(amps, "row", axis=0, tiled=True)
    table = dense_tiles(ints, task_cd, task_ab, task_count[0])
    partial_sum = ladder_term(whole, table)
    summed = sum_by_axis(partial_sum, COL, 0)
    return summed.astype(jnp.bfloat16)


def solution(mesh):
    finer = Mesh(mesh.devices.reshape(mesh.shape["row"], 8, 4), ("row", "col_0", "col_1"))
    in_specs = (P("row", COL, None), P(ROW_COL, None, None), P(ROW_COL), P(ROW_COL), P(ROW_COL))
    out_specs = P(COL, "row", None)
    return jax.shard_map(
        shards, mesh=finer, in_specs=in_specs, out_specs=out_specs, check_vma=False
    )
```

profile of v0, /device:TPU:8, one launch (start us, length us, event | category | flops | bytes accessed | tf_op | source)
XLA Modules:
  0.0 192.2 jit_solution(13895775385929147668)
XLA Ops:
  6.5 0.0 all-gather.2.cloned.1.call-start
  6.5 1.9 %copy.13 = bf16[128,8,256]{2,0,1:T(8,128)(2,1)} copy(bf16[128,8,256]{2,1,0:T(8,128)(2,1)} %param.5) | data formatting | bytes 1048576 | tf_op args[0]
  8.5 0.0 all-gather.2.cloned.1.call-update
  8.5 0.0 reduce-scatter.3.cloned.1.call-start
  9.2 0.7 multiply_add_fusion
  9.9 0.1 fusion.13
  10.0 0.1 reshape.35
  10.1 0.1 select_reduce_fusion
  10.2 0.1 reduce_sum.14
  10.3 8.6 %gather_fusion = bf16[64,256,256]{2,1,0:T(8,128)(2,1)} fusion(bf16[64,256,256]{2,1,0:T(8,128)(2,1)} %param.6, s32[1024]{0:T(1024)S(1)} %pad_clamp_fusion), kind=kCustom, calls=%fused_computation | custom fusion | bytes 16777472 | tf_op jit(solution)/shard_map/jit(_take)/gather | solution.py:28
  19.0 11.6 %copy.12 = bf16[8,8,256,256]{2,3,1,0:T(8,128)(2,1)} copy(bf16[8,8,256,256]{3,2,1,0:T(8,128)(2,1)} %bitcast.17) | data formatting | bytes 16777216 | tf_op jit(solution)/shard_map/jit(_take)/gather | solution.py:28
  30.6 15.1 %all-gather.2.cloned.1.call-done = bf16[1024,8,256]{2,0,1:T(8,128)(2,1)} async-done(((bf16[128,8,256]{2,0,1:T(8,128)(2,1)}), bf16[1024,8,256]{2,0,1:T(8,128)(2,1)}) %all-gather.2.cloned.1.call-update) | async-done | bytes 4194320 | tf_op jit(solution)/shard_map/all_gather | solution.py:37
  45.7 14.5 %fusion.7 = f32[1024,8,256]{0,2,1:T(8,128)} fusion(bf16[1024,8,256]{2,0,1:T(8,128)(2,1)} %all-gather.2.cloned.1.call-done, bf16[8,8,256,256]{2,3,1,0:T(8,128)(2,1)} %copy.12, pred[8,8]{1,0:T(8,128)(4,1)S(1)} %compare_and_fusion, bf16[8,8]{1,0:T(8,128)(2,1)S(1)} %reshape.35), kind=kOutput, calls=%fused_computation.8 | convolution fusion | flops 8598323200 | bytes 20971712 | tf_op jit(solution)/shard_map/nkt,aktu->nau/dot_general | solution.py:33
  60.2 0.0 reduce-scatter.3.cloned.1.call-update
  60.2 0.0 reduce-scatter.5.cloned.1.call-start
  60.2 96.0 %reduce-scatter.3.cloned.1.call-done = f32[128,8,256]{0,2,1:T(8,128)} async-done(((f32[1024,8,256]{0,2,1:T(8,128)}), f32[128,8,256]{0,2,1:T(8,128)}) %reduce-scatter.3.cloned.1.call-update) | async-done | bytes 1048592 | tf_op jit(solution)/shard_map/reduce_scatter | solution.py:15
  156.3 2.7 %copy.14 = f32[128,8,256]{2,1,0:T(8,128)} copy(f32[128,8,256]{0,2,1:T(8,128)} %reduce-scatter.3.cloned.1.call-done) | data formatting | bytes 2097152 | tf_op jit(solution)/shard_map/reduce_scatter | solution.py:15
  158.9 0.0 reduce-scatter.5.cloned.1.call-update
  159.0 25.1 %reduce-scatter.5.cloned.1.call-done = f32[32,8,256]{2,1,0:T(8,128)} async-done(((f32[128,8,256]{2,1,0:T(8,128)}), f32[32,8,256]{2,1,0:T(8,128)}) %reduce-scatter.5.cloned.1.call-update) | async-done | bytes 262160 | tf_op jit(solution)/shard_map/reduce_scatter | solution.py:15
  184.0 1.6 convert_element_type.15
  (5 shorter events, 0.0 us)
Async XLA Ops:
  6.5 39.1 %all-gather.2.cloned.1.call-start = ((), (), s32[]{:S(2)}) async-start(), calls=%async_computation.2 | async-start | bytes 4718592 | tf_op jit(solution)/shard_map/all_gather | solution.py:37
  8.5 147.8 %reduce-scatter.3.cloned.1.call-start = ((), (), s32[]{:S(2)}) async-start(), calls=%async_computation.3 | async-start | bytes 9437184 | tf_op jit(solution)/shard_map/reduce_scatter | solution.py:15
  60.2 123.8 %reduce-scatter.5.cloned.1.call-start = ((), (), s32[]{:S(2)}) async-start(), calls=%async_computation.4 | async-start | bytes 1310720 | tf_op jit(solution)/shard_map/reduce_scatter | solution.py:15
Sparse Core Ops, SparseCore 0:
  9.2 36.4 all-gather.1
  60.3 95.9 reduce-scatter.2
  159.1 24.8 reduce-scatter.4
where the time goes:
time: 193 us; the launch traced here: 192 us
  waiting for transfers between devices  136 us (70%)
  local copies, waits for them, and re-layouts  25 us (13%)
  matrix products  14.5 us (8%)
  between operations  13.8 us (7%)
  other arithmetic  2.57 us (1%)
    reduce_scatter x2, waiting for transfers between devices, sum_by_axis(): value = lax.psum_scatter(value, axis, scatter_dimension=dim, tiled=True)  121 us
    gather x2, local copies, waits for them, and re-layouts, dense_tiles(): jnp.take(ints, found, axis=0)  20.3 us
    all_gather x1, waiting for transfers between devices, shards(): whole = lax.all_gather(amps, 'row', axis=0, tiled=True)  15.1 us
    dot_general x1, matrix products, ladder_term(): jnp.einsum('nkt,aktu->nau', rows_amps, table, preferred_element_type=jnp....  14.5 us
  transfers between devices with their start and end apart: 3, of which 3 were waited for; matrix products, arithmetic and copies ran while one was open for 11% of the time, Pallas kernels for 0%

commit v1 on v0

--- a/solution.py
+++ b/solution.py
@@ -34,7 +34,8 @@
 
 
 def shards(amps, ints, task_cd, task_ab, task_count):
-    whole = lax.all_gather(amps, "row", axis=0, tiled=True)
+    sent = jnp.stack([amps] * lax.axis_size("row"))
+    whole = jnp.concatenate(lax.all_to_all(sent, "row", 0, 0), axis=0)
     table = dense_tiles(ints, task_cd, task_ab, task_count[0])
     partial_sum = ladder_term(whole, table)
     summed = sum_by_axis(partial_sum, COL, 0)

time: 193 us -> 213 us (1.10)
  waiting for transfers between devices: 136 us -> 151 us
  other arithmetic: 2.57 us -> 9.36 us
  starting transfers between devices: 0.09 us -> 6.68 us
  local copies, waits for them, and re-layouts: 25 us -> 19.6 us
  matrix products: 14.5 us -> 11.2 us
    all_to_all x0 -> x1, waiting for transfers between devices: none -> 31.2 us  [shards(): whole = jnp.concatenate(lax.all_to_all(sent, 'row', 0, 0), axis=0)]
    all_gather x1 -> x0, waiting for transfers between devices: 15.1 us -> none  [shards(): whole = lax.all_gather(amps, 'row', axis=0, tiled=True)]
    gather x2 -> x1, local copies, waits for them, and re-layouts: 20.3 us -> 8.66 us  [dense_tiles(): jnp.take(ints, found, axis=0)]
    mul x0 -> x1, other arithmetic: none -> 7.49 us  [dense_tiles(): jnp.take(ints, found, axis=0)]
    all_to_all x0 -> x1, starting transfers between devices: none -> 6.64 us  [shards(): whole = jnp.concatenate(lax.all_to_all(sent, 'row', 0, 0), axis=0)]
    dot_general x1, matrix products: 14.5 us -> 11.2 us  [ladder_term(): jnp.einsum('nkt,aktu->nau', rows_amps, table, preferred_element_type=jnp....]
    all_to_all x0 -> x1, local copies, waits for them, and re-layouts: none -> 2.61 us  [shards(): whole = jnp.concatenate(lax.all_to_all(sent, 'row', 0, 0), axis=0)]
    another operation x0 -> x1, local copies, waits for them, and re-layouts: none -> 2.49 us  [shards(): sent = jnp.stack([amps] * lax.axis_size('row'))]
  transfers between devices with their start and end apart: 3 -> 3, of which waited for: 3 -> 3; matrix products, arithmetic and copies ran while one was open for 11% -> 8% of each run, Pallas kernels for 0% -> 0%
where the time goes in v1:
time: 213 us; the launch traced here: 212 us
  waiting for transfers between devices  151 us (71%)
  local copies, waits for them, and re-layouts  19.6 us (9%)
  between operations  14.1 us (7%)
  matrix products  11.2 us (5%)
  other arithmetic  9.36 us (4%)
  starting transfers between devices  6.68 us (3%)
    reduce_scatter x2, waiting for transfers between devices, sum_by_axis(): value = lax.psum_scatter(value, axis, scatter_dimension=dim, tiled=True)  120 us
    all_to_all x1, waiting for transfers between devices, shards(): whole = jnp.concatenate(lax.all_to_all(sent, 'row', 0, 0), axis=0)  31.2 us
    dot_general x1, matrix products, ladder_term(): jnp.einsum('nkt,aktu->nau', rows_amps, table, preferred_element_type=jnp....  11.2 us
    gather x1, local copies, waits for them, and re-layouts, dense_tiles(): jnp.take(ints, found, axis=0)  8.66 us
    mul x1, other arithmetic, dense_tiles(): jnp.take(ints, found, axis=0)  7.49 us
    all_to_all x1, starting transfers between devices, shards(): whole = jnp.concatenate(lax.all_to_all(sent, 'row', 0, 0), axis=0)  6.64 us
  transfers between devices with their start and end apart: 3, of which 3 were waited for; matrix products, arithmetic and copies ran while one was open for 8% of the time, Pallas kernels for 0%

profile of v1, /device:TPU:8, one launch (start us, length us, event | category | flops | bytes accessed | tf_op | source)
XLA Modules:
  0.0 212.4 jit_solution(1730093701405811569)
XLA Ops:
  6.5 0.0 copy-start.2
  6.5 0.0 copy-start.1
  6.5 1.2 copy.13
  7.7 2.5 %stack.2 = bf16[8,128,8,256]{3,1,2,0:T(8,128)(2,1)} broadcast(bf16[128,8,256]{2,0,1:T(8,128)(2,1)S(1)} %copy.13), dimensions={1,2,3} | broadcast | bytes 4718592 | tf_op jit(solution)/shard_map/stack | solution.py:37
  10.2 6.6 %all-to-all-start = ((bf16[8,128,8,256]{3,1,2,0:T(8,128)(2,1)}), bf16[8,128,8,256]{3,1,2,0:T(8,128)(2,1)}, u32[]{:S(2)}, u32[]{:S(2)}) async-start(bf16[8,128,8,256]{3,1,2,0:T(8,128)(2,1)} %stack.2), calls=%async_computation | async-start | bytes 8388608 | tf_op jit(solution)/shard_map/all_to_all | solution.py:38
  16.8 0.0 reduce-scatter.3.cloned.1.call-start
  17.5 0.0 copy-done.2
  17.5 0.0 copy-done.1
  17.5 0.1 fusion.1
  17.7 0.1 select_reduce_fusion
  17.8 8.7 %gather_fusion = bf16[64,256,256]{2,1,0:T(8,128)(2,1)} fusion(bf16[64,256,256]{2,1,0:T(8,128)(2,1)} %param.6, s32[1024]{0:T(1024)S(1)} %pad_clamp_fusion), kind=kCustom, calls=%fused_computation | custom fusion | bytes 16777472 | tf_op jit(solution)/shard_map/jit(_take)/gather | solution.py:28
  26.5 7.5 %select_multiply_fusion = bf16[64,256,256]{2,1,0:T(8,128)(2,1)} fusion(bf16[64,256,256]{2,1,0:T(8,128)(2,1)} %gather_fusion, pred[64]{0:T(512)(128)(4,1)S(1)} %compare_and_fusion, bf16[64]{0:T(256)(128)(2,1)S(1)} %convert_element_type.10), kind=kLoop, calls=%fused_computation.1 | loop fusion | flops 8388608 | bytes 16777408 | tf_op jit(solution)/shard_map/mul | solution.py:28
  34.0 31.2 %all-to-all-done = bf16[8,128,8,256]{3,1,2,0:T(8,128)(2,1)} async-done(((bf16[8,128,8,256]{3,1,2,0:T(8,128)(2,1)}), bf16[8,128,8,256]{3,1,2,0:T(8,128)(2,1)}, u32[]{:S(2)}, u32[]{:S(2)}) %all-to-all-start) | async-done | bytes 4194336 | tf_op jit(solution)/shard_map/all_to_all | solution.py:38
  65.2 0.0 copy-start
  65.2 2.6 %copy.14 = bf16[8,128,8,256]{3,1,0,2:T(8,128)(2,1)S(1)} copy(bf16[8,128,8,256]{3,1,2,0:T(8,128)(2,1)} %all-to-all-done) | data formatting | bytes 8388608 | tf_op jit(solution)/shard_map/all_to_all | solution.py:38
  67.8 2.0 copy-done
  69.8 11.2 %convolution_bitcast_fusion = f32[1024,8,256]{0,2,1:T(8,128)} fusion(bf16[8,8,256,256]{3,2,1,0:T(8,128)(2,1)S(1)} %bitcast.17, bf16[1024,8,256,1]{2,0,1,3:T(8,128)(2,1)S(1)} %bitcast.18), kind=kOutput, calls=%fused_computation.2 | convolution fusion | flops 8589934592 | bytes 20971520 | tf_op jit(solution)/shard_map/nkt,aktu->nau/dot_general | solution.py:33
  81.0 0.0 reduce-scatter.3.cloned.1.call-update
  81.0 0.0 reduce-scatter.5.cloned.1.call-start
  81.1 95.2 %reduce-scatter.3.cloned.1.call-done = f32[128,8,256]{0,2,1:T(8,128)} async-done(((f32[1024,8,256]{0,2,1:T(8,128)}), f32[128,8,256]{0,2,1:T(8,128)}) %reduce-scatter.3.cloned.1.call-update) | async-done | bytes 1048592 | tf_op jit(solution)/shard_map/reduce_scatter | solution.py:15
  176.3 2.6 %copy.16 = f32[128,8,256]{2,1,0:T(8,128)} copy(f32[128,8,256]{0,2,1:T(8,128)} %reduce-scatter.3.cloned.1.call-done) | data formatting | bytes 2097152 | tf_op jit(solution)/shard_map/reduce_scatter | solution.py:15
  178.9 0.0 reduce-scatter.5.cloned.1.call-update
  178.9 25.1 %reduce-scatter.5.cloned.1.call-done = f32[32,8,256]{2,1,0:T(8,128)} async-done(((f32[128,8,256]{2,1,0:T(8,128)}), f32[32,8,256]{2,1,0:T(8,128)}) %reduce-scatter.5.cloned.1.call-update) | async-done | bytes 262160 | tf_op jit(solution)/shard_map/reduce_scatter | solution.py:15
  204.0 1.6 convert_element_type.11
  (6 shorter events, 0.0 us)
Async XLA Ops:
  6.5 11.0 %copy-start.2 = (s32[64]{0:T(128)S(1)}, s32[64]{0:T(128)}, u32[]{:S(2)}) copy-start(s32[64]{0:T(128)} %param.8) | copy-start | bytes 772
  6.5 11.0 %copy-start.1 = (s32[64]{0:T(128)S(1)}, s32[64]{0:T(128)}, u32[]{:S(2)}) copy-start(s32[64]{0:T(128)} %param.7) | copy-start | bytes 772
  10.2 55.0 %all-to-all-start = ((bf16[8,128,8,256]{3,1,2,0:T(8,128)(2,1)}), bf16[8,128,8,256]{3,1,2,0:T(8,128)(2,1)}, u32[]{:S(2)}, u32[]{:S(2)}) async-start(bf16[8,128,8,256]{3,1,2,0:T(8,128)(2,1)} %stack.2), calls=%async_computation | async-start | bytes 8388608 | tf_op jit(solution)/shard_map/all_to_all | solution.py:38
  16.8 159.4 %reduce-scatter.3.cloned.1.call-start = ((), (), s32[]{:S(2)}) async-start(), calls=%async_computation.3 | async-start | bytes 9437184 | tf_op jit(solution)/shard_map/reduce_scatter | solution.py:15
  65.2 4.6 %copy-start = (bf16[64,256,256]{2,1,0:T(8,128)(2,1)S(1)}, bf16[64,256,256]{2,1,0:T(8,128)(2,1)}, u32[]{:S(2)}) copy-start(bf16[64,256,256]{2,1,0:T(8,128)(2,1)} %select_multiply_fusion) | copy-start | bytes 25165828
  81.0 122.9 %reduce-scatter.5.cloned.1.call-start = ((), (), s32[]{:S(2)}) async-start(), calls=%async_computation.4 | async-start | bytes 1310720 | tf_op jit(solution)/shard_map/reduce_scatter | solution.py:15
Sparse Core Ops, SparseCore 0:
  81.2 95.0 reduce-scatter.2
  179.0 24.8 reduce-scatter.4
